TPU v7x, 128 devices: a whole 4x4x4 slice. The times are simulated.
128 devices in a mesh: px: 16 (over x, z), py: 8 (over y, core).
Axes of the slice: x: 4, y: 4, z: 4, core: 2. Of those that a mesh axis runs over, the one named last changes fastest.
Arguments:
- state: float32 [16, 8, 8192, 256], P('px', 'py'), may hold values from -6 to 6
- prop_base: float32 [256, 256], replicated, may hold values from -0.375 to 0.375
- prop_height: float32 [256, 256], replicated, may hold values from -0.375 to 0.375
- restrict: float32 [256, 128], replicated, may hold values from -0.375 to 0.375
- lift: float32 [128, 256], replicated, may hold values from -0.5 to 0.5
- layer_id: int32 [16, 8, 8192], P('px', 'py'), may hold values from 0 to 2
- heights: int32 [16, 8, 8192], P('px', 'py'), may hold values from 1 to 4
- degree: int32 [16, 8, 8192], P('px', 'py'), may hold values from 1 to 4
- send_rows: int32 [16, 8, 4, 512], P('px', 'py'), may hold values from 0 to 8191
- recv_rows: int32 [16, 8, 4, 512], P('px', 'py'), may hold values from 0 to 8191
- move_src: int32 [16, 8, 128], P('px', 'py'), may hold values from 0 to 8191, as said below
- move_dst: int32 [16, 8, 128], P('px', 'py'), may hold values from 0 to 127, as said below
- move_slot: int32 [16, 8, 128], P('px', 'py'), may hold values from 0 to 8191, as said below
Outputs:
- new_state: float32 [16, 8, 8192, 256], P('px', 'py')
Inputs may be any that keep to these rules, and one draw needn't show every extreme that they name: `move_src`: on each partition the 128 slots are distinct. `move_dst`: each partition hands exactly 2 elements to each of 64 other partitions and none to the rest, and receives exactly 2 elements from each of 64 partitions. `move_slot`: the slots at which a partition's arriving elements land are exactly its own move_src slots, each once.
All inputs are finite; a program needn't handle non-finite values.
Results may differ from a plain program's by a relative error of at most 0.0001.
Values sent between devices are 32-bit elements; how exact they have to be, the bound alone decides.
A program may use at most 128 MiB of HBM per device.

v0:
```python
import functools

import jax
import jax.numpy as jnp
from jax import lax
from jax.experimental import pallas as pl
from jax.experimental.pallas import tpu as pltpu
from jax.sharding import PartitionSpec as P

MESH = pl.DeviceIdType.MESH
F32 = jnp.float32
BF16 = jnp.bfloat16
LANES = 128
ROWS = 512


def split(value):
    high = value.astype(BF16)
    low = (value - high.astype(F32)).astype(BF16)
    return high, low


def pieces(value):
    high, low = split(value)
    return jnp.concatenate([high, low, high], axis=1)


def weights(value):
    high, low = split(value)
    return jnp.concatenate([high, high, low], axis=0)


def product(left, right):
    return jnp.dot(left, right, preferred_element_type=F32)


def column(row):
    return jnp.transpose(jnp.broadcast_to(row, (LANES, LANES)))


def gather_kernel(state, meta, send_idx, recv_idx, rows_out, rows_meta, recv_meta, all_meta, held, held_meta, sems, meta_sem):
    chunks = sems.shape[0]
    size = held.shape[0] // chunks
    for chunk in range(chunks):
        part = pl.ds(chunk * size, size)
        pltpu.make_async_copy(state.at[part], held.at[part], sems.at[chunk]).start()

    def spread(block, carry):
        held_meta[pl.ds(pl.multiple_of(block * LANES, LANES), LANES), :] = column(meta[pl.ds(block, 1), :])
        return carry

    lax.fori_loop(0, meta.shape[0], spread, 0)
    out_copy = pltpu.make_async_copy(held_meta, all_meta, meta_sem)
    out_copy.start()

    def take_meta(step, carry):
        first = pl.multiple_of(step * 16, 16)
        for lane in range(16):
            row = recv_idx[first + lane]
            recv_meta[pl.ds(first + lane, 1), :] = held_meta[pl.ds(row, 1), :]
        return carry

    lax.fori_loop(0, recv_meta.shape[0] // 16, take_meta, 0)
    for chunk in range(chunks):
        part = pl.ds(chunk * size, size)
        pltpu.make_async_copy(state.at[part], held.at[part], sems.at[chunk]).wait()

    def take(step, carry):
        first = pl.multiple_of(step * 16, 16)
        for lane in range(16):
            row = send_idx[first + lane]
            rows_out[pl.ds(first + lane, 1), :] = held[pl.ds(row, 1), :]
            rows_meta[pl.ds(first + lane, 1), :] = held_meta[pl.ds(row, 1), :]
        return carry

    lax.fori_loop(0, rows_out.shape[0] // 16, take, 0)
    out_copy.wait()


def layers_kernel(
    parts_x,
    parts_y,
    layers,
    windows,
    state,
    all_meta,
    rows_in,
    rows_meta,
    recv_meta,
    send_ids,
    recv_ids,
    slots,
    base,
    height,
    restrict,
    lift,
    bulk_out,
    correction,
    moved_out,
    slots_out,
    rows,
    held,
    held_meta,
    match,
    trace,
    arrived,
    arrived_pieces,
    prop_w,
    restrict_w,
    lift_w,
    move_out,
    move_in,
    slot_in,
    send_sem,
    recv_sem,
    state_sem,
    meta_sem,
    bulk_sem,
    slot_send,
    slot_recv,
    move_send,
    move_recv,
):
    px, py = lax.axis_index("px"), lax.axis_index("py")
    parts = parts_x * parts_y
    me = px * parts_y + py
    width = rows.shape[1]
    sent = trace.shape[1]
    side = sent // 4
    moves = rows.shape[0] - sent
    blocks = held.shape[0] // ROWS

    barrier = pltpu.get_barrier_semaphore()

    def greet(step, carry):
        other = lax.rem(me + step, parts)
        pl.semaphore_signal(barrier, inc=1, device_id=(other // parts_y, lax.rem(other, parts_y)), device_id_type=MESH)
        return carry

    lax.fori_loop(1, parts, greet, 0)

    def block_of(ref, block):
        return ref.at[pl.ds(pl.multiple_of(block * ROWS, ROWS), ROWS)]

    state_in = [
        pltpu.make_async_copy(state, held, state_sem),
        pltpu.make_async_copy(all_meta, held_meta, meta_sem),
    ]
    for copy in state_in:
        copy.start()

    def neighbour(side_index):
        dx = jnp.where(side_index == 0, 1, jnp.where(side_index == 1, -1, 0))
        dy = jnp.where(side_index == 2, 1, jnp.where(side_index == 3, -1, 0))
        x, y = px + dx, py + dy
        exists = (x >= 0) & (x < parts_x) & (y >= 0) & (y < parts_y)
        return x, y, exists

    def source_exists(side_index):
        dx = jnp.where(side_index == 0, -1, jnp.where(side_index == 1, 1, 0))
        dy = jnp.where(side_index == 2, -1, jnp.where(side_index == 3, 1, 0))
        x, y = px + dx, py + dy
        return (x >= 0) & (x < parts_x) & (y >= 0) & (y < parts_y)

    def trace_copy(layer, side_index, x, y):
        part = pl.ds(pl.multiple_of(side_index * side, side), side)
        return pltpu.make_async_remote_copy(
            src_ref=trace.at[layer, part],
            dst_ref=arrived.at[layer, part],
            send_sem=send_sem.at[layer, side_index],
            recv_sem=recv_sem.at[layer, side_index],
            device_id=(x, y),
            device_id_type=MESH,
        )

    def send_side(layer, side_index):
        x, y, exists = neighbour(side_index)

        @pl.when(exists)
        def _():
            trace_copy(layer, side_index, x, y).start()

    restrict_w[...] = weights(restrict[...])

    def first_trace(side_index, carry):
        part = pl.ds(pl.multiple_of(side_index * side, side), side)
        own = rows_in[part, :]
        rows[part, :] = own
        trace[0, part, :] = product(pieces(own), restrict_w[...])
        return carry

    lax.fori_loop(0, 4, first_trace, 0)
    pl.semaphore_wait(barrier, parts - 1)
    for side_index in range(4):
        send_side(0, side_index)

    def slot_copy(other):
        return pltpu.make_async_remote_copy(
            src_ref=slots.at[other],
            dst_ref=slot_in.at[me],
            send_sem=slot_send,
            recv_sem=slot_recv,
            device_id=(other // parts_y, lax.rem(other, parts_y)),
            device_id_type=MESH,
        )

    def move_copy(other):
        return pltpu.make_async_remote_copy(
            src_ref=move_out.at[other],
            dst_ref=move_in.at[me],
            send_sem=move_send,
            recv_sem=move_recv,
            device_id=(other // parts_y, lax.rem(other, parts_y)),
            device_id_type=MESH,
        )

    def send_slots(step, carry):
        slot_copy(lax.rem(me + step, parts)).start()
        return carry

    lax.fori_loop(1, parts, send_slots, 0)
    slot_in[pl.ds(me, 1)] = jnp.full((1, 1, LANES), held.shape[0], jnp.int32)
    move_in[pl.ds(me, 1)] = jnp.zeros((1, 4, LANES), F32)

    for side_index in range(4):

        @pl.when(jnp.logical_not(source_exists(side_index)))
        def _():
            for layer in range(layers):
                arrived[layer, pl.ds(side_index * side, side), :] = jnp.zeros((side, LANES), F32)

    rows[pl.ds(sent, moves), :] = rows_in[pl.ds(sent, moves), :]
    correction[...] = jnp.zeros_like(correction)
    prop_w[:, pl.ds(0, width)] = weights(base[...])
    prop_w[:, pl.ds(width, width)] = weights(height[...])
    lift_w[...] = weights(lift[...])

    def build_match(block, carry):
        ids = column(send_ids[pl.ds(block, 1), :])
        part = pl.ds(pl.multiple_of(block * LANES, LANES), LANES)
        for group in range(sent // LANES):
            same = ids == recv_ids[pl.ds(group, 1), :]
            match[part, pl.ds(group * LANES, LANES)] = jnp.where(same, 1.0, 0.0).astype(BF16)
        return carry

    lax.fori_loop(0, rows.shape[0] // LANES, build_match, 0)

    def advance(old, combined, meta, layer):
        both = product(pieces(combined), prop_w[...])
        scale = ((meta >> 2) & 7).astype(F32) * 0.25
        active = (meta >> 5) * (width // 4)
        pitched = (meta & 3) <= layer
        lane = lax.broadcasted_iota(jnp.int32, meta.shape, 1)
        halves = []
        for start in range(0, width, LANES):
            value = both[:, start : start + LANES] + scale * both[:, width + start : width + start + LANES]
            value = jnp.where(lane + start < active, value, 0.0)
            halves.append(jnp.where(pitched, value, old[:, start : start + LANES]))
        return jnp.concatenate(halves, axis=1)

    def bulk_copy(block):
        return pltpu.make_async_copy(block_of(held, block), block_of(bulk_out, block), bulk_sem.at[block])

    def bulk_block(block, carry):
        part = pl.ds(pl.multiple_of(block * ROWS, ROWS), ROWS)
        meta = held_meta[part, :]

        def one(layer, value):
            value = held[part, :]
            held[part, :] = advance(value, value, meta, layer)
            return 0

        lax.fori_loop(0, layers, one, 0)
        bulk_copy(block).start()
        return carry

    for copy in state_in:
        copy.wait()

    def compact(part, layer):
        match_rows = match[part, :]
        inflow = product(match_rows, arrived_pieces[...])
        inflow = inflow[:, :LANES] + inflow[:, LANES:]
        lifted = product(pieces(inflow), lift_w[...])
        old = rows[part, :]
        new = advance(old, old + lifted, rows_meta[part, :], layer)
        rows[part, :] = new
        return new

    def layer_step(layer, carry):
        first = jnp.where(layer == 0, 0, jnp.where(layer == 1, windows[0], windows[1]))
        last = jnp.where(layer == 0, windows[0], jnp.where(layer == 1, windows[1], windows[2]))
        lax.fori_loop(first, last, bulk_block, 0)
        for side_index in range(4):

            @pl.when(source_exists(side_index))
            def _():
                trace_copy(layer, side_index, px, py).wait_recv()

        def cut(side_index, carry):
            part = pl.ds(pl.multiple_of(side_index * side, side), side)
            high, low = split(arrived[layer, part, :])
            arrived_pieces[part, pl.ds(0, LANES)] = high
            arrived_pieces[part, pl.ds(LANES, LANES)] = low
            return carry

        lax.fori_loop(0, 4, cut, 0)

        @pl.when(layer < layers - 1)
        def _():
            def one_side(side_index, carry):
                part = pl.ds(pl.multiple_of(side_index * side, side), side)
                new = compact(part, layer)
                trace[layer + 1, part, :] = product(pieces(new), restrict_w[...])
                send_side(layer + 1, side_index)
                return carry

            lax.fori_loop(0, 4, one_side, 0)

        leaving = compact(pl.ds(sent, moves), layer)

        @pl.when(layer == layers - 1)
        def _():
            for place in range(2):
                for half in range(2):
                    move_out[:, 2 * place + half, :] = leaving[
                        place * parts : (place + 1) * parts, half * LANES : (half + 1) * LANES
                    ]

            def send_moves(step, carry):
                move_copy(lax.rem(me + step, parts)).start()
                return carry

            lax.fori_loop(1, parts, send_moves, 0)

        def correct(side_index, carry):
            part = pl.ds(pl.multiple_of(side_index * side, side), side)
            high = arrived_pieces[part, pl.ds(0, LANES)]
            low = arrived_pieces[part, pl.ds(LANES, LANES)]
            lifted = product(jnp.concatenate([high, low, high], axis=1), lift_w[...])
            old = correction[part, :]
            correction[part, :] = advance(old, old + lifted, recv_meta[part, :], layer)
            return carry

        lax.fori_loop(0, 4, correct, 0)
        return carry

    lax.fori_loop(0, layers, layer_step, 0)
    lax.fori_loop(windows[2], blocks, bulk_block, 0)

    def finish_bulk(block, carry):
        bulk_copy(block).wait()
        return carry

    lax.fori_loop(0, blocks, finish_bulk, 0)
    for side_index in range(4):
        x, y, exists = neighbour(side_index)

        @pl.when(exists)
        def _():
            for layer in range(layers):
                trace_copy(layer, side_index, x, y).wait_send()

    def whole(src, dst, sends, receives):
        return pltpu.make_async_remote_copy(
            src_ref=src.at[pl.ds(0, parts - 1)],
            dst_ref=dst.at[pl.ds(0, parts - 1)],
            send_sem=sends,
            recv_sem=receives,
            device_id=(px, py),
            device_id_type=MESH,
        )

    whole(slots, slot_in, slot_send, slot_recv).wait()
    whole(move_out, move_in, move_send, move_recv).wait()
    moved_out[...] = move_in[...]
    slots_out[...] = slot_in[...]


def scatter_kernel(bulk, correction, moved, recv_idx, repeats, slots, out, held, sems, out_sems):
    chunks = sems.shape[0]
    count = out.shape[0]
    size = count // chunks
    width = out.shape[1]
    for chunk in range(chunks):
        part = pl.ds(chunk * size, size)
        pltpu.make_async_copy(bulk.at[part], held.at[part], sems.at[chunk]).start()
    for chunk in range(chunks):
        part = pl.ds(chunk * size, size)
        pltpu.make_async_copy(bulk.at[part], held.at[part], sems.at[chunk]).wait()

    def add(step, carry):
        first = pl.multiple_of(step * 8, 8)

        @pl.when(repeats[step] == 0)
        def _():
            rows = [recv_idx[first + lane] for lane in range(8)]
            sums = [held[pl.ds(row, 1), :] + correction[pl.ds(first + lane, 1), :] for lane, row in enumerate(rows)]
            for row, value in zip(rows, sums):
                held[pl.ds(row, 1), :] = value

        @pl.when(repeats[step] != 0)
        def _():
            for lane in range(8):
                row = recv_idx[first + lane]
                held[pl.ds(row, 1), :] = held[pl.ds(row, 1), :] + correction[pl.ds(first + lane, 1), :]

        return carry

    lax.fori_loop(0, correction.shape[0] // 8, add, 0)

    def land(step, carry):
        for inner in range(4):
            source = step * 4 + inner
            for place in range(2):
                row = slots[source * 2 + place]
                halves = [moved[source, pl.ds(2 * place + half, 1), :] for half in range(width // LANES)]
                held[pl.ds(row, 1), :] = jnp.concatenate(halves, axis=1)
        return carry

    lax.fori_loop(0, moved.shape[0] // 4, land, 0)
    for chunk in range(chunks):
        part = pl.ds(chunk * size, size)
        pltpu.make_async_copy(held.at[part], out.at[part], out_sems.at[chunk]).start()
    for chunk in range(chunks):
        part = pl.ds(chunk * size, size)
        pltpu.make_async_copy(held.at[part], out.at[part], out_sems.at[chunk]).wait()


VMEM = pl.BlockSpec(memory_space=pltpu.VMEM)
SMEM = pl.BlockSpec(memory_space=pltpu.SMEM)
ANY = pl.BlockSpec(memory_space=pl.ANY)
LIMIT = 60 * 1024 * 1024


def local(
    state,
    prop_base,
    prop_height,
    restrict,
    lift,
    layer_id,
    heights,
    degree,
    send_rows,
    recv_rows,
    move_src,
    move_dst,
    move_slot,
):
    parts_x, parts_y = lax.axis_size("px"), lax.axis_size("py")
    parts = parts_x * parts_y
    current = state[0, 0]
    count, width = current.shape
    layers = 3
    recv_list = recv_rows[0, 0].reshape(-1)
    sent = recv_list.shape[0]
    moves = 2 * parts
    meta = (layer_id[0, 0] + 4 * heights[0, 0] + 32 * degree[0, 0]).astype(F32).reshape(-1, LANES)
    meta = meta.astype(jnp.int32)

    target, leaving, landing = move_dst[0, 0], move_src[0, 0], move_slot[0, 0]
    items = target.shape[0]
    order = lax.broadcasted_iota(jnp.int32, (items, items), 1) < lax.broadcasted_iota(jnp.int32, (items, items), 0)
    place = jnp.sum(((target[:, None] == target[None, :]) & order).astype(jnp.int32), axis=1)
    key = place * parts + target
    chosen = lax.broadcasted_iota(jnp.int32, (moves, items), 0) == key[None, :]
    move_idx = jnp.sum(jnp.where(chosen, leaving[None, :], 0), axis=1)
    move_to = count + jnp.sum(jnp.where(chosen, landing[None, :] - count, 0), axis=1)
    slots = jnp.pad(move_to.reshape(2, parts).T, ((0, 0), (0, LANES - 2)))[:, None, :]
    send_idx = jnp.concatenate([send_rows[0, 0].reshape(-1), move_idx])
    total = sent + moves

    rows, rows_meta, recv_meta, all_meta = pl.pallas_call(
        gather_kernel,
        name="gather_rows",
        out_shape=(
            jax.ShapeDtypeStruct((total, width), F32),
            jax.ShapeDtypeStruct((total, LANES), jnp.int32),
            jax.ShapeDtypeStruct((sent, LANES), jnp.int32),
            jax.ShapeDtypeStruct((count, LANES), jnp.int32),
        ),
        in_specs=[ANY, VMEM, SMEM, SMEM],
        out_specs=(VMEM, VMEM, VMEM, ANY),
        scratch_shapes=[
            pltpu.VMEM((count, width), F32),
            pltpu.VMEM((count, LANES), jnp.int32),
            pltpu.SemaphoreType.DMA((4,)),
            pltpu.SemaphoreType.DMA,
        ],
        compiler_params=pltpu.CompilerParams(vmem_limit_bytes=LIMIT),
    )(current, meta, send_idx, recv_list)

    blocks = count // ROWS
    windows = (blocks * 5 // 16, blocks * 9 // 16, blocks * 13 // 16)
    bulk, correction, moved, slots_in = pl.pallas_call(
        functools.partial(layers_kernel, parts_x, parts_y, layers, windows),
        name="layers",
        out_shape=(
            jax.ShapeDtypeStruct((count, width), F32),
            jax.ShapeDtypeStruct((sent, width), F32),
            jax.ShapeDtypeStruct((parts, 4, LANES), F32),
            jax.ShapeDtypeStruct((parts, 1, LANES), jnp.int32),
        ),
        in_specs=[ANY, ANY] + [VMEM] * 10,
        out_specs=(ANY, VMEM, VMEM, VMEM),
        scratch_shapes=[
            pltpu.VMEM((total, width), F32),
            pltpu.VMEM((count, width), F32),
            pltpu.VMEM((count, LANES), jnp.int32),
            pltpu.VMEM((total, sent), BF16),
            pltpu.VMEM((layers, sent, LANES), F32),
            pltpu.VMEM((layers, sent, LANES), F32),
            pltpu.VMEM((sent, 2 * LANES), BF16),
            pltpu.VMEM((3 * width, 2 * width), BF16),
            pltpu.VMEM((3 * width, LANES), BF16),
            pltpu.VMEM((3 * LANES, width), BF16),
            pltpu.VMEM((parts, 4, LANES), F32),
            pltpu.VMEM((parts, 4, LANES), F32),
            pltpu.VMEM((parts, 1, LANES), jnp.int32),
            pltpu.SemaphoreType.DMA((layers, 4)),
            pltpu.SemaphoreType.DMA((layers, 4)),
            pltpu.SemaphoreType.DMA,
            pltpu.SemaphoreType.DMA,
            pltpu.SemaphoreType.DMA((blocks,)),
            pltpu.SemaphoreType.DMA,
            pltpu.SemaphoreType.DMA,
            pltpu.SemaphoreType.DMA,
            pltpu.SemaphoreType.DMA,
        ],
        compiler_params=pltpu.CompilerParams(vmem_limit_bytes=LIMIT, collective_id=0, has_side_effects=True),
    )(
        current,
        all_meta,
        rows,
        rows_meta,
        recv_meta,
        send_idx.astype(F32).reshape(-1, LANES),
        recv_list.astype(F32).reshape(-1, LANES),
        slots,
        prop_base,
        prop_height,
        restrict,
        lift,
    )

    groups = recv_list.reshape(-1, 8)
    twins = jnp.sum((groups[:, :, None] == groups[:, None, :]).astype(jnp.int32), axis=(1, 2))
    repeats = (twins > 8).astype(jnp.int32)
    result = pl.pallas_call(
        scatter_kernel,
        name="scatter_rows",
        out_shape=jax.ShapeDtypeStruct((count, width), F32),
        in_specs=[ANY, VMEM, VMEM, SMEM, SMEM, SMEM],
        out_specs=ANY,
        scratch_shapes=[
            pltpu.VMEM((count + 8, width), F32),
            pltpu.SemaphoreType.DMA((4,)),
            pltpu.SemaphoreType.DMA((4,)),
        ],
        compiler_params=pltpu.CompilerParams(vmem_limit_bytes=LIMIT),
    )(bulk, correction, moved, recv_list, repeats, slots_in[:, 0, :2].reshape(-1))
    return result[None, None]


def solution(mesh):
    in_specs = (
        P("px", "py", None, None),
        P(),
        P(),
        P(),
        P(),
        P("px", "py", None),
        P("px", "py", None),
        P("px", "py", None),
        P("px", "py", None, None),
        P("px", "py", None, None),
        P("px", "py", None),
        P("px", "py", None),
        P("px", "py", None),
    )
    out_specs = P("px", "py", None, None)
    return jax.shard_map(local, mesh=mesh, in_specs=in_specs, out_specs=out_specs, check_vma=False)
```

profile of v0, /device:TPU:1, one launch (start us, length us, event | category | flops | bytes accessed | tf_op | source)
XLA Modules:
  0.0 139.7 jit_solution(9875634487006899356)
XLA Ops:
  0.0 0.9 convert_reduce_fusion.1
  0.9 0.7 multiply_add_fusion
  1.6 0.7 add_bitcast_fusion.1
  2.2 0.8 select_reduce_fusion
  3.0 0.7 copy.18
  3.7 0.6 convert_bitcast_fusion
  4.3 1.3 copy.19
  5.6 1.5 %convert_convert_fusion = s32[1,1,8192]{2,1,0:T(1,128)} fusion(s32[1,1,8192]{2,1,0:T(1,128)} %param.20, s32[1,1,8192]{2,1,0:T(1,128)} %param.18, s32[1,1,8192]{2,1,0:T(1,128)} %param.19), kind=kLoop, calls=%fused_computation.8 | loop fusion | flops 49152 | bytes 131072 | tf_op jit(solution)/shard_map/convert_element_type | solution.py:460
  7.1 0.0 copy-start
  7.1 20.8 %gather_rows.1 = (f32[2304,256]{1,0:T(8,128)}, s32[2304,128]{1,0:T(8,128)}, s32[2048,128]{1,0:T(8,128)}, s32[8192,128]{1,0:T(8,128)}) custom-call(f32[8192,256]{1,0:T(8,128)} %bitcast.18, s32[64,128]{1,0:T(8,128)} %bitcast.22, s32[2304]{0:T(1024)} %get-tuple-element.24.send_idx, s32[2048]{0:T(1024)} %bitcast.24), custom_call_target="tpu_custom_call" | custom-call | tf_op jit(solution)/shard_map/gather_rows/pallas_call | solution.py:474
  27.9 0.1 copy.15
  28.0 0.6 pad.4
  28.6 0.0 copy-done
  28.6 0.6 convert_element_type.40.recv_ids
  29.2 86.7 %layers.1 = (f32[8192,256]{1,0:T(8,128)}, f32[2048,256]{1,0:T(8,128)}, f32[128,4,128]{2,1,0:T(4,128)}, s32[128,1,128]{2,1,0:T(1,128)}) custom-call(f32[8192,256]{1,0:T(8,128)} %bitcast.19, s32[8192,128]{1,0:T(8,128)} %get-tuple-element.13.all_meta, f32[2304,256]{1,0:T(8,128)} %get-tuple-element.14.rows_in, s32[2304,128]{1,0:T(8,128)} %get-tuple-element.15.rows_meta, ...), custom_call_target="tpu_custom_call" | custom-call | tf_op jit(solution)/shard_map/layers/pallas_call | solution.py:496
  115.9 1.0 slice_reduce_fusion
  116.9 0.7 reshape_squeeze.11.slots
  117.6 0.1 eq.44
  117.7 0.1 copy.16
  117.8 0.5 compare_convert_fusion.repeats
  118.4 21.4 %scatter_rows.1 = f32[8192,256]{1,0:T(8,128)} custom-call(f32[8192,256]{1,0:T(8,128)} %get-tuple-element.17.bulk, f32[2048,256]{1,0:T(8,128)} %get-tuple-element.18.correction, f32[128,4,128]{2,1,0:T(4,128)} %get-tuple-element.19.moved, s32[2048]{0:T(1024)} %bitcast.25, s32[256]{0:T(256)} %compare_convert_fusion.repeats, s32[256]{0:T(256)} %reshape_squeeze.11.slots), custom_call_target="tpu_custom_call" | custom-call | tf_op jit(solution)/shard_map/scatter_rows/pallas_call | solution.py:550
  (3 shorter events, 0.0 us)
Async XLA Ops:
  7.1 21.5 %copy-start = (s32[1,1,4,512]{3,2,1,0:T(4,128)S(1)}, s32[1,1,4,512]{3,2,1,0:T(4,128)}, u32[]{:S(2)}) copy-start(s32[1,1,4,512]{3,2,1,0:T(4,128)} %param.22) | copy-start | bytes 24580
where the time goes:
time: 140 us
  Pallas kernels  129 us (92%)
  other arithmetic  5.68 us (4%)
  local copies, waits for them, and re-layouts  5.19 us (4%)
    pallas_call x1, Pallas kernels, local(): pl.pallas_call(functools.partial(layers_kernel, parts_x, parts_y, layers,...  86.7 us
    pallas_call x1, Pallas kernels, local(): pl.pallas_call(scatter_kernel, name='scatter_rows', out_shape=jax.ShapeDt...  21.4 us
    pallas_call x1, Pallas kernels, local(): pl.pallas_call(gather_kernel, name='gather_rows', out_shape=(jax.ShapeDty...  20.8 us

commit v1 on v0

v1 whole, which is shorter than its diff:
```python
import functools

import jax
import jax.numpy as jnp
from jax import lax
from jax.experimental import pallas as pl
from jax.experimental.pallas import tpu as pltpu
from jax.sharding import PartitionSpec as P

MESH = pl.DeviceIdType.MESH
F32 = jnp.float32
BF16 = jnp.bfloat16
LANES = 128
ROWS = 1024
MARK = 1 << 20
BATCH = 16
PLACE_RECV = 24
SPARE = 8


def split(value):
    high = value.astype(BF16)
    return high, (value - high.astype(F32)).astype(BF16)


def pieces(values):
    pairs = [split(value) for value in values]
    high = [pair[0] for pair in pairs]
    return jnp.concatenate(high + [pair[1] for pair in pairs] + high, axis=1)


def weights(value):
    high, low = split(value)
    return jnp.concatenate([high, high, low], axis=0)


def product(left, right):
    return jnp.dot(left, right, preferred_element_type=F32)


def column(row):
    return jnp.transpose(jnp.broadcast_to(row, (LANES, LANES)))


def layers_kernel(
    parts_x,
    parts_y,
    layers,
    windows,
    state,
    meta,
    send_rows,
    recv_rows,
    target,
    leaving,
    landing,
    base,
    height,
    restrict,
    lift,
    bulk_out,
    correction_out,
    moved_out,
    slots_out,
    recv_out,
    rows,
    held,
    recv_meta,
    correction,
    match,
    trace,
    arrived,
    arrived_pieces,
    prop_w,
    restrict_w,
    lift_w,
    through_w,
    places,
    place_list,
    flat_ids,
    flat_recv,
    slots,
    move_out,
    move_in,
    slot_in,
    send_sem,
    recv_sem,
    state_sem,
    list_sem,
    bulk_sem,
    correction_sem,
    slot_send,
    slot_recv,
    move_send,
    move_recv,
):
    px, py = lax.axis_index("px"), lax.axis_index("py")
    parts = parts_x * parts_y
    me = px * parts_y + py
    count, width = state.shape[0] * 8, state.shape[2]
    sent = trace.shape[1]
    side = sent // 4
    moves = 2 * parts
    halves = width // LANES
    groups = halves + 1
    held_flat = held.reshape(held.shape[0] * 8 * groups, LANES)
    rows_flat = rows.reshape(rows.shape[0] * 8 * groups, LANES)
    blocks = count // ROWS
    chunks = state_sem.shape[0]

    barrier = pltpu.get_barrier_semaphore()

    def greet(step, carry):
        other = lax.rem(me + step, parts)
        pl.semaphore_signal(barrier, inc=1, device_id=(other // parts_y, lax.rem(other, parts_y)), device_id_type=MESH)
        return carry

    def state_copy(chunk, half):
        part = pl.ds(chunk * (count // 8 // chunks), count // 8 // chunks)
        return pltpu.make_async_copy(
            state.at[part, :, pl.ds(half * LANES, LANES)], held.at[part, half], state_sem.at[chunk, half]
        )

    for chunk in range(chunks):
        for half in range(halves):
            state_copy(chunk, half).start()
    lax.fori_loop(1, parts, greet, 0)

    def neighbour(side_index):
        dx = jnp.where(side_index == 0, 1, jnp.where(side_index == 1, -1, 0))
        dy = jnp.where(side_index == 2, 1, jnp.where(side_index == 3, -1, 0))
        x, y = px + dx, py + dy
        exists = (x >= 0) & (x < parts_x) & (y >= 0) & (y < parts_y)
        return x, y, exists

    def source_exists(side_index):
        dx = jnp.where(side_index == 0, -1, jnp.where(side_index == 1, 1, 0))
        dy = jnp.where(side_index == 2, -1, jnp.where(side_index == 3, 1, 0))
        x, y = px + dx, py + dy
        return (x >= 0) & (x < parts_x) & (y >= 0) & (y < parts_y)

    def trace_copy(layer, side_index, x, y):
        part = pl.ds(pl.multiple_of(side_index * side, side), side)
        return pltpu.make_async_remote_copy(
            src_ref=trace.at[layer, part],
            dst_ref=arrived.at[layer, part],
            send_sem=send_sem.at[layer, side_index],
            recv_sem=recv_sem.at[layer, side_index],
            device_id=(x, y),
            device_id_type=MESH,
        )

    def send_side(layer, side_index):
        x, y, exists = neighbour(side_index)

        @pl.when(exists)
        def _():
            trace_copy(layer, side_index, x, y).start()

    lane = lax.broadcasted_iota(jnp.int32, (LANES, LANES), 1)
    item = lax.broadcasted_iota(jnp.int32, (LANES, LANES), 0)
    to = column(target[...])
    earlier = (to == target[...]) & (item < lane)
    place = column(jnp.sum(jnp.where(earlier, 1, 0), axis=0, keepdims=True))
    source_of = column(leaving[...])
    landing_of = column(landing[...]) - count
    spread_slots = []
    for which in range(2):
        chosen = (to == lane) & (place == which)
        ids = jnp.sum(jnp.where(chosen, source_of, 0), axis=0, keepdims=True)
        flat_ids[pl.ds(sent // LANES + which, 1), :] = ids
        slot = count + jnp.sum(jnp.where(chosen, landing_of, 0), axis=0, keepdims=True)
        spread_slots.append(column(slot))
        flat_ids[pl.ds(sent // LANES + which, 1), :] = ids.astype(jnp.int32)
    for index in range(sent // LANES):
        side_index, start = index * LANES // side, index * LANES % side
        flat_ids[pl.ds(index, 1), :] = send_rows[side_index : side_index + 1, start : start + LANES]
        flat_recv[pl.ds(index, 1), :] = recv_rows[side_index : side_index + 1, start : start + LANES]
    places[pl.ds(0, flat_ids.shape[0]), :] = flat_ids[...] + (groups - 1) * 8 * (flat_ids[...] >> 3)
    received = flat_recv[...]
    places[pl.ds(PLACE_RECV, received.shape[0]), :] = received + (groups - 1) * 8 * (received >> 3)
    list_copy = pltpu.make_async_copy(places, place_list, list_sem)
    list_copy.start()
    slots[:, 0, :] = jnp.where(lane == 0, spread_slots[0], spread_slots[1])

    place_in_batch = lax.broadcasted_iota(jnp.int32, received.shape, 1) & (BATCH - 1)
    marks = jnp.zeros(received.shape, F32)
    for shift in range(1, BATCH):
        same = (received == pltpu.roll(received, shift, 1)) & (place_in_batch >= shift)
        marks = jnp.where(same, 1.0, marks)
    shift = 1
    while shift < BATCH:
        marks = jnp.maximum(marks, pltpu.roll(marks, shift, 1))
        shift *= 2
    spots = received + (halves - 1) * 8 * (received >> 3)
    recv_out[...] = spots + jnp.where((place_in_batch == BATCH - 1) & (marks > 0.5), MARK, 0)

    restrict_high, restrict_low = split(restrict[...])
    restrict_w[:, pl.ds(0, LANES)] = restrict_high
    restrict_w[:, pl.ds(LANES, LANES)] = restrict_low

    def spread(block, carry):
        part = pl.ds(pl.multiple_of(block * (LANES // 8), LANES // 8), LANES // 8)
        held[part, halves] = column(meta[pl.ds(block, 1), :]).reshape(LANES // 8, 8, LANES)
        return carry

    lax.fori_loop(0, meta.shape[0], spread, 0)

    def traced(values):
        pairs = [split(value) for value in values]
        high = jnp.concatenate([pair[0] for pair in pairs], axis=1)
        low = jnp.concatenate([pair[1] for pair in pairs], axis=1)
        both = product(high, restrict_w[...])
        return both[:, :LANES] + both[:, LANES:] + product(low, restrict_w[:, pl.ds(0, LANES)])

    def read(ref, first, size, which):
        part = pl.ds(pl.multiple_of(first // 8, size // 8), size // 8)
        return ref[part, which].reshape(size, LANES)

    def write(ref, first, size, values):
        part = pl.ds(pl.multiple_of(first // 8, size // 8), size // 8)
        for which, value in enumerate(values):
            ref[part, which] = value.reshape(size // 8, 8, LANES)

    def read_row(ref, first, size):
        return [read(ref, first, size, half) for half in range(halves)]

    list_copy.wait()
    for chunk in range(chunks):
        for half in range(halves):
            state_copy(chunk, half).wait()

    def take(line, carry):
        into = rows_flat.at[pl.ds(pl.multiple_of(line * (LANES * groups), LANES * groups), LANES * groups + SPARE * 8)]
        for inner in range(LANES):
            spot = inner // 8 * 8 * groups + inner % 8
            into[pl.ds(spot, groups, stride=8), :] = held_flat[pl.ds(place_list[line, inner], groups, stride=8), :]
        return carry

    for side_index in range(4):
        lax.fori_loop(side_index * (side // LANES), (side_index + 1) * (side // LANES), take, 0)
        trace[0, pl.ds(side_index * side, side), :] = traced(read_row(rows, side_index * side, side))
        if side_index == 0:
            pl.semaphore_wait(barrier, parts - 1)
        send_side(0, side_index)

    def slot_copy(other):
        return pltpu.make_async_remote_copy(
            src_ref=slots.at[other],
            dst_ref=slot_in.at[me],
            send_sem=slot_send,
            recv_sem=slot_recv,
            device_id=(other // parts_y, lax.rem(other, parts_y)),
            device_id_type=MESH,
        )

    def move_copy(other):
        return pltpu.make_async_remote_copy(
            src_ref=move_out.at[other],
            dst_ref=move_in.at[me],
            send_sem=move_send,
            recv_sem=move_recv,
            device_id=(other // parts_y, lax.rem(other, parts_y)),
            device_id_type=MESH,
        )

    def send_slots(step, carry):
        slot_copy(lax.rem(me + step, parts)).start()
        return carry

    lax.fori_loop(1, parts, send_slots, 0)
    slot_in[pl.ds(me, 1)] = jnp.full((1, 1, LANES), count, jnp.int32)
    move_in[pl.ds(me, 1)] = jnp.zeros((1, 4, LANES), F32)

    lax.fori_loop(sent // LANES, (sent + moves) // LANES, take, 0)

    def take_meta(line, carry):
        into = recv_meta.at[pl.ds(pl.multiple_of(line * LANES, LANES), LANES)]
        for inner in range(LANES):
            place = place_list[line + PLACE_RECV, inner]
            into[inner : inner + 1, :] = held_flat[pl.ds(place + 8 * halves, 1), :]
        return carry

    lax.fori_loop(0, sent // LANES, take_meta, 0)
    for side_index in range(4):

        @pl.when(jnp.logical_not(source_exists(side_index)))
        def _():
            for layer in range(layers):
                arrived[layer, pl.ds(side_index * side, side), :] = jnp.zeros((side, LANES), F32)

    prop_w[:, pl.ds(0, width)] = weights(base[...])
    prop_w[:, pl.ds(width, width)] = weights(height[...])
    lift_w[...] = weights(lift[...])
    through = product(pieces([lift[:, half * LANES : (half + 1) * LANES] for half in range(halves)]), prop_w[...])
    through_w[...] = weights(through)

    def match_rows_of(row, part):
        ids = column(row)
        for group in range(sent // LANES):
            same = ids == flat_recv[group : group + 1, :]
            match[part, pl.ds(group * LANES, LANES)] = jnp.where(same, 1.0, 0.0).astype(BF16)

    def build_match(block, carry):
        match_rows_of(flat_ids[pl.ds(block, 1), :], pl.ds(pl.multiple_of(block * LANES, LANES), LANES))
        return carry

    lax.fori_loop(0, (sent + moves) // LANES, build_match, 0)

    def finish(both, old, packed, layer):
        info = packed.astype(jnp.int32)
        scale = ((info >> 2) & 7).astype(F32) * 0.25
        active = (info >> 5) * (width // 4)
        pitched = (info & 3) <= layer
        lane = lax.broadcasted_iota(jnp.int32, info.shape, 1)
        values = []
        for half in range(halves):
            start = half * LANES
            value = both[:, start : start + LANES] + scale * both[:, width + start : width + start + LANES]
            value = jnp.where(lane + start < active, value, 0.0)
            values.append(jnp.where(pitched, value, 0.0 if old is None else old[half]))
        return values

    def advance(old, combined, packed, layer):
        return finish(product(pieces(combined), prop_w[...]), old, packed, layer)

    def bulk_copy(block):
        part = pl.ds(pl.multiple_of(block * (ROWS // 8), ROWS // 8), ROWS // 8)
        return pltpu.make_async_copy(held.at[part, pl.ds(0, halves)], bulk_out.at[part], bulk_sem.at[block])

    def bulk_block(block, carry):
        first = block * ROWS

        def one(layer, carry):
            values = read_row(held, first, ROWS)
            write(held, first, ROWS, advance(values, values, read(held, first, ROWS, halves), layer))
            return carry

        lax.fori_loop(0, layers, one, 0)
        bulk_copy(block).start()
        return carry

    def plus(values, added):
        return [value + added[:, half * LANES : (half + 1) * LANES] for half, value in enumerate(values)]

    def compact(first, size, layer):
        inflow = product(match[pl.ds(pl.multiple_of(first, size), size), :], arrived_pieces[...])
        lifted = product(pieces([inflow[:, :LANES] + inflow[:, LANES:]]), lift_w[...])
        old = read_row(rows, first, size)
        new = advance(old, plus(old, lifted), read(rows, first, size, halves), layer)
        write(rows, first, size, new)
        return new

    def correction_copy(side_index):
        part = pl.ds(pl.multiple_of(side_index * (side // 8), side // 8), side // 8)
        return pltpu.make_async_copy(correction.at[part], correction_out.at[part], correction_sem.at[side_index])

    def layer_step(layer, carry):
        first = jnp.where(layer == 0, 0, jnp.where(layer == 1, windows[0], windows[1]))
        last = jnp.where(layer == 0, windows[0], jnp.where(layer == 1, windows[1], windows[2]))
        lax.fori_loop(first, last, bulk_block, 0)
        for side_index in range(4):

            @pl.when(source_exists(side_index))
            def _():
                trace_copy(layer, side_index, px, py).wait_recv()

        def cut(side_index, carry):
            part = pl.ds(pl.multiple_of(side_index * side, side), side)
            high, low = split(arrived[layer, part, :])
            arrived_pieces[part, pl.ds(0, LANES)] = high
            arrived_pieces[part, pl.ds(LANES, LANES)] = low
            return carry

        lax.fori_loop(0, 4, cut, 0)

        @pl.when(layer < layers - 1)
        def _():
            def two_sides(pair, carry):
                part = pl.ds(pl.multiple_of(pair * 2 * side, 2 * side), 2 * side)
                trace[layer + 1, part, :] = traced(compact(pair * 2 * side, 2 * side, layer))
                send_side(layer + 1, 2 * pair)
                send_side(layer + 1, 2 * pair + 1)
                return carry

            lax.fori_loop(0, 2, two_sides, 0)

        leaving_rows = compact(sent, moves, layer)

        @pl.when(layer == layers - 1)
        def _():
            for which in range(2):
                for half in range(2):
                    move_out[:, 2 * which + half, :] = leaving_rows[half][which * parts : (which + 1) * parts]

            def send_moves(step, carry):
                move_copy(lax.rem(me + step, parts)).start()
                return carry

            lax.fori_loop(1, parts, send_moves, 0)

        def correct(pair, carry):
            part = pl.ds(pl.multiple_of(pair * 2 * side, 2 * side), 2 * side)
            high = arrived_pieces[part, pl.ds(0, LANES)]
            low = arrived_pieces[part, pl.ds(LANES, LANES)]
            triple = jnp.concatenate([high, low, high], axis=1)
            info = recv_meta[part, :]
            first = pair * 2 * side

            @pl.when(layer == 0)
            def _():
                write(correction, first, 2 * side, finish(product(triple, through_w[...]), None, info, layer))

            @pl.when(layer > 0)
            def _():
                old = read_row(correction, first, 2 * side)
                new = advance(old, plus(old, product(triple, lift_w[...])), info, layer)
                write(correction, first, 2 * side, new)

            @pl.when(layer == layers - 1)
            def _():
                correction_copy(2 * pair).start()
                correction_copy(2 * pair + 1).start()

            return carry

        lax.fori_loop(0, 2, correct, 0)
        return carry

    lax.fori_loop(0, layers, layer_step, 0)
    lax.fori_loop(windows[2], blocks, bulk_block, 0)

    def whole(src, dst, sends, receives):
        return pltpu.make_async_remote_copy(
            src_ref=src.at[pl.ds(0, parts - 1)],
            dst_ref=dst.at[pl.ds(0, parts - 1)],
            send_sem=sends,
            recv_sem=receives,
            device_id=(px, py),
            device_id_type=MESH,
        )

    whole(slots, slot_in, slot_send, slot_recv).wait()
    landed = jnp.transpose(slot_in[:, 0, :])[:2, :]
    slots_out[...] = landed + (halves - 1) * 8 * (landed >> 3)

    def finish_bulk(block, carry):
        bulk_copy(block).wait()
        return carry

    lax.fori_loop(0, blocks, finish_bulk, 0)
    for side_index in range(4):
        correction_copy(side_index).wait()
        x, y, exists = neighbour(side_index)

        @pl.when(exists)
        def _():
            for layer in range(layers):
                trace_copy(layer, side_index, x, y).wait_send()

    whole(move_out, move_in, move_send, move_recv).wait()
    moved_out[pl.ds(0, parts)] = move_in[...]


def scatter_kernel(bulk, correction, moved, recv_list, slots, out, held, added, sems, added_sem, out_sems):
    chunks = sems.shape[0]
    tiles, halves = bulk.shape[:2]
    size = tiles // chunks
    held_flat = held.reshape(held.shape[0] * halves * 8, LANES)
    added_flat = added.reshape(added.shape[0] * halves * 8, LANES)

    def bulk_copy(chunk):
        part = pl.ds(chunk * size, size)
        return pltpu.make_async_copy(bulk.at[part], held.at[part], sems.at[chunk])

    def out_copy(chunk, half):
        part = pl.ds(chunk * size, size)
        return pltpu.make_async_copy(
            held.at[part, half], out.at[part, :, pl.ds(half * LANES, LANES)], out_sems.at[chunk, half]
        )

    added_copy = pltpu.make_async_copy(correction, added.at[pl.ds(0, correction.shape[0])], added_sem)
    added_copy.start()
    for chunk in range(chunks):
        bulk_copy(chunk).start()
    added_copy.wait()
    for chunk in range(chunks):
        bulk_copy(chunk).wait()

    def add(line, carry):
        for batch in range(LANES // BATCH):
            first = pl.multiple_of((line * LANES + batch * BATCH) * halves, BATCH * halves)
            source = added_flat.at[pl.ds(first, BATCH * halves + SPARE * 8)]
            start = batch * BATCH
            last = recv_list[line, start + BATCH - 1]

            @pl.when(last < MARK)
            def _():
                spots = [recv_list[line, start + inner] for inner in range(BATCH)]
                sums = []
                for inner, spot in enumerate(spots):
                    own = source[pl.ds(inner // 8 * 8 * halves + inner % 8, halves, stride=8), :]
                    sums.append(held_flat[pl.ds(spot, halves, stride=8), :] + own)
                for spot, value in zip(spots, sums):
                    held_flat[pl.ds(spot, halves, stride=8), :] = value

            @pl.when(last >= MARK)
            def _():
                def one(inner, carry):
                    spot = recv_list[line, start + inner] & (MARK - 1)
                    own = added_flat[pl.ds(first + inner // 8 * 8 * halves + lax.rem(inner, 8), halves, stride=8), :]
                    held_flat[pl.ds(spot, halves, stride=8), :] = held_flat[pl.ds(spot, halves, stride=8), :] + own
                    return carry

                lax.fori_loop(0, BATCH, one, 0)

        return carry

    lax.fori_loop(0, recv_list.shape[0], add, 0)

    for which in range(2):
        for source in range(slots.shape[1]):
            spot = slots[which, source]
            held_flat[pl.ds(spot, halves, stride=8), :] = moved[source, pl.ds(halves * which, halves), :]
    for chunk in range(chunks):
        for half in range(halves):
            out_copy(chunk, half).start()
    for chunk in range(chunks):
        for half in range(halves):
            out_copy(chunk, half).wait()


VMEM = pl.BlockSpec(memory_space=pltpu.VMEM)
SMEM = pl.BlockSpec(memory_space=pltpu.SMEM)
ANY = pl.BlockSpec(memory_space=pl.ANY)
LIMIT = 60 * 1024 * 1024


def local(
    state,
    prop_base,
    prop_height,
    restrict,
    lift,
    layer_id,
    heights,
    degree,
    send_rows,
    recv_rows,
    move_src,
    move_dst,
    move_slot,
):
    parts_x, parts_y = lax.axis_size("px"), lax.axis_size("py")
    parts = parts_x * parts_y
    current = state[0, 0]
    count, width = current.shape
    halves = width // LANES
    layers = 3
    to_send, to_take = send_rows[0, 0], recv_rows[0, 0]
    sent = to_take.size
    total = sent + 2 * parts
    meta = (layer_id[0, 0] + 4 * heights[0, 0] + 32 * degree[0, 0]).astype(F32).reshape(-1, LANES)
    blocks = count // ROWS
    windows = (blocks // 8, blocks * 3 // 8, blocks * 5 // 8)
    bulk, correction, moved, slots, marked = pl.pallas_call(
        functools.partial(layers_kernel, parts_x, parts_y, layers, windows),
        name="layers",
        out_shape=(
            jax.ShapeDtypeStruct((count // 8, halves, 8, LANES), F32),
            jax.ShapeDtypeStruct((sent // 8, halves, 8, LANES), F32),
            jax.ShapeDtypeStruct((parts + SPARE, 4, LANES), F32),
            jax.ShapeDtypeStruct((2, parts), jnp.int32),
            jax.ShapeDtypeStruct((sent // LANES, LANES), jnp.int32),
        ),
        in_specs=[ANY] + [VMEM] * 10,
        out_specs=(ANY, ANY, VMEM, VMEM, VMEM),
        scratch_shapes=[
            pltpu.VMEM((total // 8 + SPARE, halves + 1, 8, LANES), F32),
            pltpu.VMEM((count // 8 + SPARE, halves + 1, 8, LANES), F32),
            pltpu.VMEM((sent + 8, LANES), F32),
            pltpu.VMEM((sent // 8, halves, 8, LANES), F32),
            pltpu.VMEM((total, sent), BF16),
            pltpu.VMEM((layers, sent, LANES), F32),
            pltpu.VMEM((layers, sent, LANES), F32),
            pltpu.VMEM((sent, 2 * LANES), BF16),
            pltpu.VMEM((3 * width, 2 * width), BF16),
            pltpu.VMEM((width, 2 * LANES), BF16),
            pltpu.VMEM((3 * LANES, width), BF16),
            pltpu.VMEM((3 * LANES, 2 * width), BF16),
            pltpu.VMEM((PLACE_RECV + sent // LANES, LANES), jnp.int32),
            pltpu.SMEM((PLACE_RECV + sent // LANES, LANES), jnp.int32),
            pltpu.VMEM((total // LANES, LANES), jnp.int32),
            pltpu.VMEM((sent // LANES, LANES), jnp.int32),
            pltpu.VMEM((parts, 1, LANES), jnp.int32),
            pltpu.VMEM((parts, 4, LANES), F32),
            pltpu.VMEM((parts, 4, LANES), F32),
            pltpu.VMEM((parts, 1, LANES), jnp.int32),
            pltpu.SemaphoreType.DMA((layers, 4)),
            pltpu.SemaphoreType.DMA((layers, 4)),
            pltpu.SemaphoreType.DMA((4, halves)),
            pltpu.SemaphoreType.DMA,
            pltpu.SemaphoreType.DMA((blocks,)),
            pltpu.SemaphoreType.DMA((4,)),
            pltpu.SemaphoreType.DMA,
            pltpu.SemaphoreType.DMA,
            pltpu.SemaphoreType.DMA,
            pltpu.SemaphoreType.DMA,
        ],
        compiler_params=pltpu.CompilerParams(vmem_limit_bytes=LIMIT, collective_id=0, has_side_effects=True),
    )(
        current.reshape(count // 8, 8, width),
        meta,
        to_send,
        to_take,
        move_dst[0],
        move_src[0],
        move_slot[0],
        prop_base,
        prop_height,
        restrict,
        lift,
    )
    result = pl.pallas_call(
        scatter_kernel,
        name="scatter_rows",
        out_shape=jax.ShapeDtypeStruct((count // 8, 8, width), F32),
        in_specs=[ANY, ANY, VMEM, SMEM, SMEM],
        out_specs=ANY,
        scratch_shapes=[
            pltpu.VMEM((count // 8 + 1 + SPARE, halves, 8, LANES), F32),
            pltpu.VMEM((sent // 8 + SPARE, halves, 8, LANES), F32),
            pltpu.SemaphoreType.DMA((4,)),
            pltpu.SemaphoreType.DMA,
            pltpu.SemaphoreType.DMA((4, halves)),
        ],
        compiler_params=pltpu.CompilerParams(vmem_limit_bytes=LIMIT),
    )(bulk, correction, moved, marked, slots)
    return result.reshape(count, width)[None, None]


def solution(mesh):
    in_specs = (
        P("px", "py", None, None),
        P(),
        P(),
        P(),
        P(),
        P("px", "py", None),
        P("px", "py", None),
        P("px", "py", None),
        P("px", "py", None, None),
        P("px", "py", None, None),
        P("px", "py", None),
        P("px", "py", None),
        P("px", "py", None),
    )
    out_specs = P("px", "py", None, None)
    return jax.shard_map(local, mesh=mesh, in_specs=in_specs, out_specs=out_specs, check_vma=False)
```

time: 140 us -> 99 us (0.71)
  Pallas kernels: 129 us -> 96.9 us
  local copies, waits for them, and re-layouts: 5.19 us -> 0 us
  other arithmetic: 5.68 us -> 1.47 us
    pallas_call x1 -> x0, Pallas kernels: 20.8 us -> none  [local(): pl.pallas_call(gather_kernel, name='gather_rows', out_shape=(jax.ShapeDty...]
    pallas_call x1, Pallas kernels: 21.4 us -> 13.4 us  [local(): pl.pallas_call(scatter_kernel, name='scatter_rows', out_shape=jax.ShapeDt...]
    pallas_call x1, Pallas kernels: 86.7 us -> 83.4 us  [local(): pl.pallas_call(functools.partial(layers_kernel, parts_x, parts_y, layers,...]
    unnamed x4 -> x0, local copies, waits for them, and re-layouts: 2 us -> none
    reduce_sum x3 -> x0, other arithmetic: 1.74 us -> none  [the longest x1 0.9 us: local(): jnp.sum(((target[:, None] == target[None, :]) & order).astype(jnp.int32),...]
where the time goes in v1:
time: 99 us; the launch traced here: 98.3 us
  Pallas kernels  96.9 us (98%)
  other arithmetic  1.47 us (1%)
    pallas_call x1, Pallas kernels, local(): pl.pallas_call(functools.partial(layers_kernel, parts_x, parts_y, layers,...  83.4 us
    pallas_call x1, Pallas kernels, local(): pl.pallas_call(scatter_kernel, name='scatter_rows', out_shape=jax.ShapeDt...  13.4 us

profile of v1, /device:TPU:1, one launch (start us, length us, event | category | flops | bytes accessed | tf_op | source)
XLA Modules:
  0.0 98.3 jit_solution(2646741844622371025)
XLA Ops:
  0.0 1.5 %add_convert_fusion = f32[1,1,8192]{2,1,0:T(1,128)} fusion(s32[1,1,8192]{2,1,0:T(1,128)} %param.20, s32[1,1,8192]{2,1,0:T(1,128)} %param.18, s32[1,1,8192]{2,1,0:T(1,128)} %param.19), kind=kLoop, calls=%fused_computation | loop fusion | flops 40960 | bytes 131072 | tf_op jit(solution)/shard_map/convert_element_type | solution.py:563
  1.5 83.4 %layers.1 = (f32[1024,2,8,128]{3,2,1,0:T(8,128)}, f32[256,2,8,128]{3,2,1,0:T(8,128)}, f32[136,4,128]{2,1,0:T(4,128)}, s32[2,128]{1,0:T(2,128)}, s32[16,128]{1,0:T(8,128)}) custom-call(f32[1024,8,256]{2,1,0:T(8,128)} %bitcast.8, f32[64,128]{1,0:T(8,128)} %bitcast.9, s32[4,512]{1,0:T(4,128)} %bitcast.10, s32[4,512]{1,0:T(4,128)} %bitcast.11, ...), custom_call_target="tpu_custom_call" | custom-call | tf_op jit(solution)/shard_map/layers/pallas_call | solution.py:566
  84.9 13.4 %scatter_rows.1 = f32[1024,8,256]{2,1,0:T(8,128)} custom-call(f32[1024,2,8,128]{3,2,1,0:T(8,128)} %get-tuple-element.10.bulk, f32[256,2,8,128]{3,2,1,0:T(8,128)} %get-tuple-element.11.correction, f32[136,4,128]{2,1,0:T(4,128)} %get-tuple-element.12.moved, s32[16,128]{1,0:T(8,128)} %get-tuple-element.13.recv_list, s32[2,128]{1,0:T(2,128)} %get-tuple-element.14.slots), custom_call_target="tpu_custom_call" | custom-call | tf_op jit(solution)/shard_map/scatter_rows/pallas_call | solution.py:624
